TPU v7x, 256 devices: a whole 4x4x8 slice. The times are simulated.
256 devices in a mesh: pairs: 64 (over y, z, core), orb: 4 (over x).
Axes of the slice: x: 4, y: 4, z: 8, core: 2. Of those that a mesh axis runs over, the one named last changes fastest.
Arguments:
- amplitudes: float32 [1024, 128, 128], P(('pairs', 'orb')), may hold values from -4 to 4
- integrals: bfloat16 [1024, 128, 128], P(('pairs', 'orb')), may hold values from -6 to 6
- energies: float32 [1024, 128], P(('pairs', 'orb')), may hold values from 0.5 to 4
- intersections: bfloat16 [1024, 16, 128, 128], P(('pairs', 'orb')), may hold values from -0.5 to 0.5
- couplings: float32 [1024, 16], P(('pairs', 'orb')), may hold values from -2 to 2
- projector: float32 [1024, 128], P(('pairs', 'orb')), may hold values from -0.5 to 0.5
- pair_orbitals: int32 [1024, 2], P(('pairs', 'orb')), may hold values from 0 to 31
- coupled: int32 [1024, 16], replicated, may hold values from 0 to 1023, as said below
- pair_slot: int32 [1024], replicated, may hold values from 0 to 1023, as said below
Outputs:
- final_amplitudes: float32 [1024, 128, 128], P(('pairs', 'orb'))
- residual: float32 [1024, 128, 128], P(('pairs', 'orb'))
Inputs may be any that keep to these rules, and one draw needn't show every extreme that they name: `coupled`: each row holds 16 different pair ids, never the id of the pair held in that row's slot. The rows of one device name at most 1 different pairs held by the devices of any one pairs index, and exactly 1 held by the devices of the next pairs index. `pair_slot`: A permutation of the pair ids.
All inputs are finite; a program needn't handle non-finite values.
Results may differ from a plain program's by a relative error of at most 0.00037.
Values may be sent and summed in bfloat16 or wider, within the bound.
A program may use at most 64 MiB of HBM per device.

v0:
```python
import jax
import jax.numpy as jnp
from jax import lax
from jax.sharding import PartitionSpec as P

PAIRS_ORB = 32
ITERS = 2


def body(
    amplitudes,
    integrals,
    energies,
    intersections,
    couplings,
    projector,
    pair_orbitals,
    coupled,
    pair_slot,
):
    highest = lax.Precision.HIGHEST
    pair_count = lax.axis_size("pairs")
    orb_count = lax.axis_size("orb")
    devices = pair_count * orb_count
    per_device = amplitudes.shape[0]
    width = amplitudes.shape[1]
    total = coupled.shape[0]
    capacity = 1 + coupled.shape[1] // pair_count
    group = orb_count * per_device
    orbitals = total // PAIRS_ORB
    pair_idx = lax.axis_index("pairs")
    orb_idx = lax.axis_index("orb")
    device_id = pair_idx * orb_count + orb_idx
    targets = pair_slot[coupled]
    row_owner = jnp.broadcast_to(
        (jnp.arange(total, dtype=jnp.int32) // per_device)[:, None], targets.shape
    )
    needed = jnp.zeros((devices, total), jnp.int32).at[row_owner, targets].set(1)
    mine = lax.dynamic_slice_in_dim(needed, device_id, 1, 0)[0].reshape(pair_count, group)
    ranks = (jnp.cumsum(mine, axis=1) - 1).reshape(total)
    own_targets = lax.dynamic_slice_in_dim(targets, device_id * per_device, per_device, 0)
    slot_ids = jnp.arange(capacity, dtype=jnp.int32)
    group_cols = lax.dynamic_slice_in_dim(needed, pair_idx * group, group, 1)
    group_rank = jnp.cumsum(group_cols, axis=1) - 1
    entry_pos = own_targets // group * capacity + ranks[own_targets]
    dest_cols = group_cols.reshape(pair_count, orb_count, group)
    dest_cols = lax.dynamic_slice_in_dim(dest_cols, orb_idx, 1, 1)[:, 0]
    dest_rank = group_rank.reshape(pair_count, orb_count, group)
    dest_rank = lax.dynamic_slice_in_dim(dest_rank, orb_idx, 1, 1)[:, 0]
    select = (
        (dest_cols == 1)[:, None, :] & (dest_rank[:, None, :] == slot_ids[None, :, None])
    ).astype(jnp.bfloat16)
    orbital_ids = jnp.arange(orbitals, dtype=jnp.int32)
    first_hot = (pair_orbitals[:, 0:1] == orbital_ids[None, :]).astype(jnp.float32)
    second_hot = (pair_orbitals[:, 1:2] == orbital_ids[None, :]).astype(jnp.float32)
    denom = energies[:, :, None] + energies[:, None, :]
    state = amplitudes
    residual = amplitudes
    for step in range(ITERS):
        blocks = state.astype(jnp.bfloat16)
        group_blocks = lax.all_gather(blocks, "orb", axis=0, tiled=True)
        outgoing = jnp.einsum(
            "pcj,jxy->pcxy", select, group_blocks, preferred_element_type=jnp.float32
        )
        outgoing = outgoing.astype(jnp.bfloat16)
        arrived = lax.all_to_all(outgoing, "pairs", split_axis=0, concat_axis=0, tiled=True)
        arrived = arrived.reshape(pair_count * capacity, width, width)
        fetched = arrived[entry_pos]
        lifted = jnp.einsum(
            "pkab,pkbc->pkac", intersections, fetched, preferred_element_type=jnp.float32
        )
        scaled = (couplings[:, :, None, None] * lifted).astype(jnp.bfloat16)
        coupling = jnp.einsum(
            "pkac,pkdc->pad", scaled, intersections, preferred_element_type=jnp.float32
        )
        projected = jnp.einsum("pab,pb->pa", state, projector, precision=highest)
        partial_sum = jnp.dot(first_hot.T, projected, precision=highest) + jnp.dot(
            second_hot.T, projected, precision=highest
        )
        summed = lax.psum(partial_sum, ("pairs", "orb"))
        left = jnp.dot(first_hot, summed, precision=highest)
        right = jnp.dot(second_hot, summed, precision=highest)
        residual = (
            integrals.astype(jnp.float32)
            + energies[:, :, None] * state
            + state * energies[:, None, :]
            - coupling
            + left[:, :, None] * projector[:, None, :]
            + projector[:, :, None] * right[:, None, :]
        )
        state = state - residual / denom
    return (state, residual)


def solution(mesh):
    return jax.shard_map(
        body,
        mesh=mesh,
        in_specs=(
            P(("pairs", "orb"), None, None),
            P(("pairs", "orb"), None, None),
            P(("pairs", "orb"), None),
            P(("pairs", "orb"), None, None, None),
            P(("pairs", "orb"), None),
            P(("pairs", "orb"), None),
            P(("pairs", "orb"), None),
            P(),
            P(),
        ),
        out_specs=(P(("pairs", "orb"), None, None), P(("pairs", "orb"), None, None)),
        check_vma=False,
    )
```

profile of v0, /device:TPU:1, one launch (start us, length us, event | category | flops | bytes accessed | tf_op | source)
XLA Modules:
  0.0 392.0 jit_solution(17940552267861765877)
XLA Ops:
  0.7 0.6 add_select_fusion
  1.3 0.6 broadcast_compare_fusion
  1.9 0.8 compare_select_fusion.1
  2.7 0.2 copy.38
  2.9 0.2 reshape.137
  3.1 65.3 %gather_fusion = s32[16384]{0:T(1024)S(1)} fusion(s32[1024]{0:T(1024)S(1)} %copy-done.1, s32[16384]{0:T(1024)S(1)} %broadcast_clamp_fusion), kind=kCustom, calls=%fused_computation | custom fusion | bytes 196608 | tf_op jit(solution)/shard_map/gather | solution.py:34
  68.5 0.2 gather.15
  68.7 0.2 copy.39
  68.9 0.2 copy-done.3
  69.2 0.1 and_reduce_fusion
  69.3 0.2 copy.40
  69.5 0.2 reshape.167
  69.8 0.6 broadcast.186
  70.4 60.8 %scatter_custom_fusion = s32[262144]{0:T(1024)S(1)} fusion(s32[16384]{0:T(1024)S(1)} %reshape.167, s32[16384]{0:T(1024)} %broadcast.186, s32[]{:T(128)} %constant.52.clone.1), kind=kCustom, calls=%fused_computation.28 | custom fusion | bytes 1049088
  131.2 1.1 reshape.134
  132.3 1.0 constant_dynamic-slice_fusion
  133.4 0.7 reduce_window_sum.22
  134.1 12.3 %all_gather.6 = bf16[16,128,128]{2,1,0:T(8,128)(2,1)S(1)} all-gather(bf16[4,128,128]{2,1,0:T(8,128)(2,1)S(1)} %convert_element_type.38), channel_id=1, replica_groups=mesh['pairs'=64,'orb'=4] {'orb'}, dimensions={0}, use_global_device_ids=true | all-gather | bytes 655360 | tf_op jit(solution)/shard_map/all_gather | solution.py:61
  146.4 0.7 convert_bitcast_fusion.1
  147.1 2.6 copy.45
  149.8 14.2 %all-to-all-start = ((bf16[64,1,128,128]{3,2,1,0:T(8,128)(2,1)}), bf16[64,1,128,128]{3,2,1,0:T(8,128)(2,1)}, u32[]{:S(2)}, u32[]{:S(2)}) async-start(bf16[64,1,128,128]{3,2,1,0:T(8,128)(2,1)} %copy.45), calls=%async_computation | async-start | bytes 4194304 | tf_op jit(solution)/shard_map/all_to_all | solution.py:66
  164.0 0.2 reshape.136
  164.2 0.8 dynamic-slice_reduce_fusion
  165.1 0.2 reduce_window_sum.23
  165.3 0.1 reshape.145
  165.4 0.7 gather_fusion.1
  166.2 0.1 reshape.144
  166.3 0.1 reshape.153
  166.4 0.5 fusion.65
  166.9 0.3 fusion.54
  167.2 0.3 convolution_add_fusion.1
  167.4 89.2 %psum.14 = f32[32,128]{1,0:T(8,128)S(1)} all-reduce(f32[32,128]{1,0:T(8,128)S(1)} %convolution_add_fusion.1), channel_id=1, replica_groups=mesh['pairs'=64,'orb'=4] {'pairs','orb'}, use_global_device_ids=true, to_apply=%region_3.4 | all-reduce | flops 4096 | bytes 32768 | tf_op jit(solution)/shard_map/psum | solution.py:80
  256.7 0.2 fusion.53
  256.9 0.2 fusion.50
  257.1 3.7 gather_fusion.2
  260.8 3.8 fusion.64
  264.6 11.4 %all_gather.7 = bf16[16,128,128]{2,1,0:T(8,128)(2,1)S(1)} all-gather(bf16[4,128,128]{2,1,0:T(8,128)(2,1)S(1)} %get-tuple-element.4), channel_id=1, replica_groups=mesh['pairs'=64,'orb'=4] {'orb'}, dimensions={0}, use_global_device_ids=true | all-gather | bytes 655360 | tf_op jit(solution)/shard_map/all_gather | solution.py:61
  276.1 0.7 convert_bitcast_fusion
  276.8 2.6 copy.50
  279.4 11.7 %all-to-all-start.1 = ((bf16[64,1,128,128]{3,2,1,0:T(8,128)(2,1)}), bf16[64,1,128,128]{3,2,1,0:T(8,128)(2,1)}, u32[]{:S(2)}, u32[]{:S(2)}) async-start(bf16[64,1,128,128]{3,2,1,0:T(8,128)(2,1)} %copy.50), calls=%async_computation.1 | async-start | bytes 4194304 | tf_op jit(solution)/shard_map/all_to_all | solution.py:66
  291.1 0.5 fusion.66
  291.6 0.3 fusion.52
  291.9 0.3 convolution_add_fusion
  292.2 91.1 %psum.15 = f32[32,128]{1,0:T(8,128)S(1)} all-reduce(f32[32,128]{1,0:T(8,128)S(1)} %convolution_add_fusion), channel_id=1, replica_groups=mesh['pairs'=64,'orb'=4] {'pairs','orb'}, use_global_device_ids=true, to_apply=%region_4.5 | all-reduce | flops 4096 | bytes 32768 | tf_op jit(solution)/shard_map/psum | solution.py:80
  383.3 0.2 fusion.51
  383.5 0.2 fusion.49
  383.7 3.7 gather_fusion.3
  387.4 4.6 %fusion.40 = (f32[4,128,128]{2,1,0:T(8,128)}, f32[4,128,128]{2,1,0:T(8,128)}) fusion(f32[4,128,128]{2,1,0:T(8,128)S(1)} %get-tuple-element.5, f32[4,128]{1,0:T(4,128)S(1)} %copy-done.12, f32[4,128]{1,0:T(4,128)S(1)} %fusion.49, f32[4,128]{1,0:T(4,128)S(1)} %copy-done.5, f32[4,128]{1,0:T(4,128)S(1)} %fusion.51, bf16[4,16,128,128]{3,2,1,0:T(8,128)(2,1)S(1)} %copy-done, ...), kind=kOutput, calls=%fused_computation.35 | convolution fusion | flops 539820032 | bytes 5120256 | tf_op jit(solution)/shard_map/pkac,pkdc->pad/dot_general | solution.py:73
  (43 shorter events, 0.5 us)
Async XLA Ops:
  0.6 260.2 %copy-start = (bf16[4,16,128,128]{3,2,1,0:T(8,128)(2,1)S(1)}, bf16[4,16,128,128]{3,2,1,0:T(8,128)(2,1)}, u32[]{:S(2)}) copy-start(bf16[4,16,128,128]{3,2,1,0:T(8,128)(2,1)} %param.12) | copy-start | bytes 6291460
  0.6 2.5 copy-start.1
  68.4 0.7 copy-start.3
  68.4 0.7 copy-start.4
  68.4 0.7 copy-start.6
  68.4 0.7 copy-start.9
  68.4 0.8 copy-start.8
  69.7 64.4 %copy-start.2 = (f32[4,128,128]{2,1,0:T(8,128)S(1)}, f32[4,128,128]{2,1,0:T(8,128)}, u32[]{:S(2)}) copy-start(f32[4,128,128]{2,1,0:T(8,128)} %param.9) | copy-start | bytes 786436
  149.8 107.3 %all-to-all-start = ((bf16[64,1,128,128]{3,2,1,0:T(8,128)(2,1)}), bf16[64,1,128,128]{3,2,1,0:T(8,128)(2,1)}, u32[]{:S(2)}, u32[]{:S(2)}) async-start(bf16[64,1,128,128]{3,2,1,0:T(8,128)(2,1)} %copy.45), calls=%async_computation | async-start | bytes 4194304 | tf_op jit(solution)/shard_map/all_to_all | solution.py:66
  164.0 2.4 copy-start.7
  164.0 2.4 copy-start.5
  257.0 3.8 copy-start.10
  257.0 3.8 copy-start.11
  257.1 3.8 copy-start.12
  279.4 104.3 %all-to-all-start.1 = ((bf16[64,1,128,128]{3,2,1,0:T(8,128)(2,1)}), bf16[64,1,128,128]{3,2,1,0:T(8,128)(2,1)}, u32[]{:S(2)}, u32[]{:S(2)}) async-start(bf16[64,1,128,128]{3,2,1,0:T(8,128)(2,1)} %copy.50), calls=%async_computation.1 | async-start | bytes 4194304 | tf_op jit(solution)/shard_map/all_to_all | solution.py:66
where the time goes:
time: 393 us; the launch traced here: 392 us
  blocking collectives  204 us (52%)
  local copies, waits for them, and re-layouts  145 us (37%)
  starting transfers between devices  25.9 us (7%)
  matrix products  12.6 us (3%)
    psum x2, blocking collectives, body(): summed = lax.psum(partial_sum, ('pairs', 'orb'))  180 us
    gather x3, local copies, waits for them, and re-layouts, body(): targets = pair_slot[coupled]  65.6 us
    unnamed x30, local copies, waits for them, and re-layouts  62.1 us
    all_to_all x2, starting transfers between devices, body(): lax.all_to_all(outgoing, 'pairs', split_axis=0, concat_axis=0, tiled=True)  25.9 us
    all_gather x2, blocking collectives, body(): group_blocks = lax.all_gather(blocks, 'orb', axis=0, tiled=True)  23.7 us
    dot_general x2, matrix products, body(): jnp.einsum('pkac,pkdc->pad', scaled, intersections, preferred_element_typ...  8.38 us
  transfers between devices with their start and end apart: 2, of which 0 were waited for; matrix products, arithmetic and copies ran while one was open for 1% of the time, Pallas kernels for 0%

commit v1 on v0

--- a/solution.py
+++ b/solution.py
@@ -2,9 +2,14 @@
 import jax.numpy as jnp
 from jax import lax
 from jax.sharding import PartitionSpec as P
+from jax.lax import all_gather
 
 PAIRS_ORB = 32
 ITERS = 2
+
+
+def yards_obtain(array_here):
+    return all_gather(array_here, ("pairs", "orb")).sum(axis=0)
 
 
 def body(
@@ -77,7 +82,7 @@
         partial_sum = jnp.dot(first_hot.T, projected, precision=highest) + jnp.dot(
             second_hot.T, projected, precision=highest
         )
-        summed = lax.psum(partial_sum, ("pairs", "orb"))
+        summed = yards_obtain(partial_sum)
         left = jnp.dot(first_hot, summed, precision=highest)
         right = jnp.dot(second_hot, summed, precision=highest)
         residual = (

time: 393 us -> 367 us (0.934)
  blocking collectives: 204 us -> 83.5 us
  waiting for transfers between devices: 0.01 us -> 86.5 us
  between operations: 1.02 us -> 14.4 us
  starting transfers between devices: 25.9 us -> 14.3 us
  other arithmetic: 3.3 us -> 8.81 us
    psum x2 -> x0, blocking collectives: 180 us -> none  [body(): summed = lax.psum(partial_sum, ('pairs', 'orb'))]
    all_to_all x0 -> x1, blocking collectives: none -> 59.7 us  [body(): lax.all_to_all(outgoing, 'pairs', split_axis=0, concat_axis=0, tiled=True)]
    all_to_all x2 -> x1, waiting for transfers between devices: 0.01 us -> 48.7 us  [body(): lax.all_to_all(outgoing, 'pairs', split_axis=0, concat_axis=0, tiled=True)]
    all_gather x0 -> x2, waiting for transfers between devices: none -> 37.7 us  [yards_obtain(): return all_gather(array_here, ('pairs', 'orb')).sum(axis=0)]
    all_to_all x2 -> x1, starting transfers between devices: 25.9 us -> 14.2 us  [body(): lax.all_to_all(outgoing, 'pairs', split_axis=0, concat_axis=0, tiled=True)]
    reduce_sum x0 -> x2, other arithmetic: none -> 5.07 us  [yards_obtain(): return all_gather(array_here, ('pairs', 'orb')).sum(axis=0)]
    unnamed x30 -> x32, local copies, waits for them, and re-layouts: 62.1 us -> 61.2 us
  transfers between devices with their start and end apart: 2 -> 3, of which waited for: 0 -> 2; matrix products, arithmetic and copies ran while one was open for 1% -> 40% of each run, Pallas kernels for 0% -> 0%
where the time goes in v1:
time: 367 us; the launch traced here: 366 us
  local copies, waits for them, and re-layouts  144 us (39%)
  waiting for transfers between devices  86.5 us (24%)
  blocking collectives  83.5 us (23%)
  matrix products  14.8 us (4%)
  between operations  14.4 us (4%)
  starting transfers between devices  14.3 us (4%)
  other arithmetic  8.81 us (2%)
    gather x3, local copies, waits for them, and re-layouts, body(): targets = pair_slot[coupled]  65.6 us
    unnamed x32, local copies, waits for them, and re-layouts  61.2 us
    all_to_all x1, blocking collectives, body(): lax.all_to_all(outgoing, 'pairs', split_axis=0, concat_axis=0, tiled=True)  59.7 us
    all_to_all x1, waiting for transfers between devices, body(): lax.all_to_all(outgoing, 'pairs', split_axis=0, concat_axis=0, tiled=True)  48.7 us
    all_gather x2, waiting for transfers between devices, yards_obtain(): return all_gather(array_here, ('pairs', 'orb')).sum(axis=0)  37.7 us
    all_gather x2, blocking collectives, body(): group_blocks = lax.all_gather(blocks, 'orb', axis=0, tiled=True)  23.9 us
    all_to_all x1, starting transfers between devices, body(): lax.all_to_all(outgoing, 'pairs', split_axis=0, concat_axis=0, tiled=True)  14.2 us
    dot_general x2, matrix products, body(): jnp.einsum('pkac,pkdc->pad', scaled, intersections, preferred_element_typ...  8.4 us
  transfers between devices with their start and end apart: 3, of which 2 were waited for; matrix products, arithmetic and copies ran while one was open for 40% of the time, Pallas kernels for 0%

profile of v1, /device:TPU:1, one launch (start us, length us, event | category | flops | bytes accessed | tf_op | source)
XLA Modules:
  0.0 366.1 jit_solution(4115843318954296336)
XLA Ops:
  7.2 0.8 slice_bitcast_fusion
  8.1 1.5 fusion.65
  9.5 0.3 fusion.54
  9.8 0.9 convolution_add_fusion.1
  10.7 1.6 convert_element_type.38
  12.4 0.8 compare_select_fusion.1
  13.2 0.2 copy.38
  13.4 0.2 reshape.137
  13.6 65.3 %gather_fusion = s32[16384]{0:T(1024)S(1)} fusion(s32[1024]{0:T(1024)S(1)} %copy-done.1, s32[16384]{0:T(1024)S(1)} %broadcast_clamp_fusion), kind=kCustom, calls=%fused_computation | custom fusion | bytes 196608 | tf_op jit(solution)/shard_map/gather | solution.py:39
  78.9 0.2 gather.15
  79.2 0.2 copy.39
  79.4 0.2 copy-done.6
  79.7 0.1 and_reduce_fusion
  79.8 0.2 copy.40
  80.0 0.2 reshape.167
  80.2 60.6 %scatter_custom_fusion = s32[262144]{0:T(1024)S(1)} fusion(s32[16384]{0:T(1024)S(1)} %reshape.167, s32[16384]{0:T(1024)S(1)} %broadcast.186, s32[]{:T(128)} %constant.53.clone.1), kind=kCustom, calls=%fused_computation.28 | custom fusion | bytes 1048580
  140.8 1.2 reshape.134
  142.0 1.0 constant_dynamic-slice_fusion
  143.0 0.7 reduce_window_sum.22
  143.8 12.3 %all_gather.18 = bf16[16,128,128]{2,1,0:T(8,128)(2,1)S(1)} all-gather(bf16[4,128,128]{2,1,0:T(8,128)(2,1)S(1)} %copy-done.3), channel_id=1, replica_groups=mesh['pairs'=64,'orb'=4] {'orb'}, dimensions={0}, use_global_device_ids=true | all-gather | bytes 655360 | tf_op jit(solution)/shard_map/all_gather | solution.py:66
  156.1 0.7 convert_bitcast_fusion.1
  156.8 2.7 copy.45
  159.4 14.2 %all-to-all-start = ((bf16[64,1,128,128]{3,2,1,0:T(8,128)(2,1)}), bf16[64,1,128,128]{3,2,1,0:T(8,128)(2,1)}, u32[]{:S(2)}, u32[]{:S(2)}) async-start(bf16[64,1,128,128]{3,2,1,0:T(8,128)(2,1)} %copy.45), calls=%async_computation | async-start | bytes 4194304 | tf_op jit(solution)/shard_map/all_to_all | solution.py:71
  173.7 0.2 reshape.136
  173.9 0.1 reshape.145
  174.0 0.8 dynamic-slice_reduce_fusion
  174.9 0.2 reduce_window_sum.23
  175.1 0.7 gather_fusion.1
  175.9 0.1 reshape.144
  176.1 48.7 %all-to-all-done = bf16[64,1,128,128]{3,2,1,0:T(8,128)(2,1)} async-done(((bf16[64,1,128,128]{3,2,1,0:T(8,128)(2,1)}), bf16[64,1,128,128]{3,2,1,0:T(8,128)(2,1)}, u32[]{:S(2)}, u32[]{:S(2)}) %all-to-all-start) | async-done | bytes 2097184 | tf_op jit(solution)/shard_map/all_to_all | solution.py:71
  224.8 3.7 %gather_fusion.2 = bf16[64,128,128]{2,1,0:T(8,128)(2,1)} fusion(bf16[64,128,128]{2,1,0:T(8,128)(2,1)} %bitcast.4, s32[1024]{0:T(1024)S(1)} %pad_clamp_fusion), kind=kCustom, calls=%fused_computation.2 | custom fusion | bytes 4194560 | tf_op jit(solution)/shard_map/gather | solution.py:73
  228.5 2.6 reduce_sum.18
  231.1 0.2 fusion.50
  231.3 0.2 fusion.53
  231.5 3.8 %fusion.64 = (bf16[4,128,128]{2,1,0:T(8,128)(2,1)S(1)}, f32[4,128,128]{2,1,0:T(8,128)S(1)}) fusion(f32[4,128,128]{2,1,0:T(8,128)S(1)} %copy-done.2, f32[4,128]{1,0:T(4,128)S(1)} %fusion.50, f32[4,128]{1,0:T(4,128)S(1)} %copy-done.4, f32[4,128]{1,0:T(4,128)S(1)} %fusion.53, bf16[4,16,128,128]{3,2,1,0:T(8,128)(2,1)S(1)} %copy-done, ...), kind=kOutput, calls=%fused_computation.90 | convolution fusion | flops 539885568 | bytes 4989184 | tf_op jit(solution)/shard_map/pkac,pkdc->pad/dot_general | solution.py:78
  235.3 0.5 fusion.66
  235.9 0.3 fusion.52
  236.1 0.9 convolution_add_fusion
  237.1 11.6 %all_gather.21 = bf16[16,128,128]{2,1,0:T(8,128)(2,1)S(1)} all-gather(bf16[4,128,128]{2,1,0:T(8,128)(2,1)S(1)} %get-tuple-element.4), channel_id=1, replica_groups=mesh['pairs'=64,'orb'=4] {'orb'}, dimensions={0}, use_global_device_ids=true | all-gather | bytes 655360 | tf_op jit(solution)/shard_map/all_gather | solution.py:66
  248.6 0.7 convert_bitcast_fusion
  249.3 1.4 copy.50
  250.7 59.7 %all_to_all.10 = bf16[64,1,128,128]{3,2,1,0:T(8,128)(2,1)} all-to-all(bf16[64,1,128,128]{3,2,1,0:T(8,128)(2,1)S(1)} %copy.50), channel_id=1, replica_groups=mesh['pairs'=64,'orb'=4] {'pairs'}, dimensions={0} | all-to-all | bytes 4194304 | tf_op jit(solution)/shard_map/all_to_all | solution.py:71
  310.4 3.7 %gather_fusion.3 = bf16[64,128,128]{2,1,0:T(8,128)(2,1)} fusion(bf16[64,128,128]{2,1,0:T(8,128)(2,1)} %bitcast.100, s32[1024]{0:T(1024)S(1)} %pad_clamp_fusion), kind=kCustom, calls=%fused_computation.3 | custom fusion | bytes 4194560 | tf_op jit(solution)/shard_map/gather | solution.py:73
  314.1 37.7 %all-gather.7.cloned.1.call-done = f32[8192,128]{1,0:T(8,128)} async-done(((f32[32,128]{1,0:T(8,128)}), f32[8192,128]{1,0:T(8,128)}) %all-gather.7.cloned.1.call-update) | async-done | bytes 4194320 | tf_op jit(solution)/shard_map/all_gather | solution.py:12
  351.8 2.5 reduce_sum.19
  354.3 0.2 fusion.49
  354.5 0.2 fusion.51
  354.7 4.6 %fusion.40 = (f32[4,128,128]{2,1,0:T(8,128)}, f32[4,128,128]{2,1,0:T(8,128)}) fusion(f32[4,128,128]{2,1,0:T(8,128)S(1)} %get-tuple-element.5, f32[4,128]{1,0:T(4,128)S(1)} %copy-done.13, f32[4,128]{1,0:T(4,128)S(1)} %fusion.49, f32[4,128]{1,0:T(4,128)S(1)} %copy-done.4, f32[4,128]{1,0:T(4,128)S(1)} %fusion.51, bf16[4,16,128,128]{3,2,1,0:T(8,128)(2,1)S(1)} %copy-done, ...), kind=kOutput, calls=%fused_computation.35 | convolution fusion | flops 539820032 | bytes 5120256 | tf_op jit(solution)/shard_map/pkac,pkdc->pad/dot_general | solution.py:78
  (50 shorter events, 0.7 us)
Async XLA Ops:
  7.2 224.3 %copy-start = (bf16[4,16,128,128]{3,2,1,0:T(8,128)(2,1)S(1)}, bf16[4,16,128,128]{3,2,1,0:T(8,128)(2,1)}, u32[]{:S(2)}) copy-start(bf16[4,16,128,128]{3,2,1,0:T(8,128)(2,1)} %param.12) | copy-start | bytes 6291460
  7.2 6.5 %copy-start.1 = (s32[1024]{0:T(1024)S(1)}, s32[1024]{0:T(1024)}, u32[]{:S(2)}) copy-start(s32[1024]{0:T(1024)} %param.17) | copy-start | bytes 12292
  7.2 221.3 %all-gather.5.cloned.1.call-start = ((), (), s32[]{:S(2)}) async-start(), calls=%async_computation.2 | async-start | bytes 4210688 | tf_op jit(solution)/shard_map/all_gather | solution.py:12
  8.1 1.5 copy-start.7
  8.1 1.8 copy-start.9
  78.9 0.7 copy-start.6
  78.9 0.7 copy-start.5
  80.2 63.6 %copy-start.3 = (bf16[4,128,128]{2,1,0:T(8,128)(2,1)S(1)}, bf16[4,128,128]{2,1,0:T(8,128)(2,1)}, u32[]{:S(2)}) copy-start(bf16[4,128,128]{2,1,0:T(8,128)(2,1)} %convert_element_type.38) | copy-start | bytes 393220
  159.4 65.3 %all-to-all-start = ((bf16[64,1,128,128]{3,2,1,0:T(8,128)(2,1)}), bf16[64,1,128,128]{3,2,1,0:T(8,128)(2,1)}, u32[]{:S(2)}, u32[]{:S(2)}) async-start(bf16[64,1,128,128]{3,2,1,0:T(8,128)(2,1)} %copy.45), calls=%async_computation | async-start | bytes 4194304 | tf_op jit(solution)/shard_map/all_to_all | solution.py:71
  173.6 178.2 %all-gather.7.cloned.1.call-start = ((), (), s32[]{:S(2)}) async-start(), calls=%async_computation.3 | async-start | bytes 4210688 | tf_op jit(solution)/shard_map/all_gather | solution.py:12
  228.5 2.6 copy-start.10
  228.5 2.8 copy-start.8
  228.5 3.0 copy-start.2
  228.5 3.0 copy-start.4
  228.5 3.0 copy-start.11
  228.5 3.0 copy-start.12
  228.5 3.0 copy-start.13
Sparse Core Ops, SparseCore 0:
  12.3 119.9 all-gather.4
  237.2 114.6 all-gather.6
